TPU v7x, 128 devices: a whole 4x4x4 slice. The times are simulated.
128 devices in a mesh: pipe: 4 (over z), seq: 16 (over y, x), cfg: 2 (over core).
Axes of the slice: x: 4, y: 4, z: 4, core: 2. Of those that a mesh axis runs over, the one named last changes fastest.
Arguments:
- hidden: bfloat16 [2, 4, 2048, 5120], P('cfg', 'pipe', 'seq'), may hold values from -6 to 6
- qkv_weight: bfloat16 [4, 5120, 3, 4096], P('pipe', None, None, 'seq'), may hold values from -1 to 1
- out_weight: bfloat16 [4, 4096, 5120], P('pipe', 'seq'), may hold values from -0.09375 to 0.09375
- qk_gain: float32 [4, 2, 4096], P('pipe', None, 'seq'), may hold values from 0 to 8
- stale_kv: bfloat16 [2, 4, 2, 4096, 4096], P('cfg', 'pipe', None, None, 'seq'), may hold values from -6 to 6
- modulation: float32 [4, 50, 3, 5120], P('pipe'), may hold values from -3 to 3
- head_mod: float32 [50, 2, 5120], replicated, may hold values from -3 to 3
- head_weight: bfloat16 [5120, 64], replicated, may hold values from -0.078125 to 0.078125
- patch_index: int32 [1], replicated, may hold values from 0 to 1
- timestep: int32 [1], replicated, may hold values from 0 to 49
Outputs:
- forwarded: bfloat16 [2, 4, 2048, 5120], P('cfg', 'pipe', 'seq')
- fresh_kv: bfloat16 [2, 4, 2, 2048, 4096], P('cfg', 'pipe', None, None, 'seq')
- guided: float32 [4, 2048, 64], P('pipe', 'seq', 'cfg')
All inputs are finite; a program needn't handle non-finite values.
Results may differ from a plain program's by a relative error of at most 0.01.
Values may be sent and summed in bfloat16 or wider, within the bound.
No kernel may reach another device: no remote copies, remote signals or barrier semaphores. Data moves between devices by JAX's collectives and lax.ppermute only.
A program may use at most 128 MiB of HBM per device.

v0:
```python
import math
import jax
import jax.numpy as jnp
from jax import lax
from jax.sharding import PartitionSpec as P

HEAD = 128
NPATCH = 2
epsilon = 1e-06
guidance = 5.0


def passed_along(block, axis, distance):
    devices = range(lax.axis_size(axis))
    route = [((i - distance) % len(devices), i) for i in devices]
    return lax.ppermute(block, axis, route)


def partner_2(shard, axis, stride):
    return lax.ppermute(shard, axis, [(i, i ^ 1 << stride) for i in range(lax.axis_size(axis))])


def modulate(inputs, shift_row, scale_row):
    values = inputs.astype(jnp.float32)
    center = jnp.mean(values, axis=-1, keepdims=True)
    spread = jnp.mean(jnp.square(values - center), axis=-1, keepdims=True)
    return (values - center) * lax.rsqrt(spread + epsilon) * (1.0 + scale_row) + shift_row


def per_device(
    hidden,
    qkv_weight,
    out_weight,
    qk_gain,
    stale_kv,
    modulation,
    head_mod,
    head_weight,
    patch_index,
    timestep,
):
    tokens_in = hidden[0, 0]
    step_row = timestep[0]
    mod_rows = lax.dynamic_index_in_dim(modulation[0], step_row, 0, keepdims=False)
    head_rows = lax.dynamic_index_in_dim(head_mod, step_row, 0, keepdims=False)
    in_weight = qkv_weight[0]
    model_width = in_weight.shape[0]
    local_width = in_weight.shape[2]
    in_weight = in_weight.reshape(model_width, 3 * local_width)
    normed = modulate(tokens_in, mod_rows[0], mod_rows[1]).astype(jnp.bfloat16)
    projections = jnp.dot(
        lax.all_gather(normed, "seq", axis=0, tiled=True),
        in_weight,
        preferred_element_type=jnp.float32,
    )
    patch_tokens = projections.shape[0]
    queries = projections[:, :local_width]
    key_cols = projections[:, local_width : 2 * local_width]
    value_cols = projections[:, 2 * local_width :]
    square_sums = lax.psum(
        (jnp.sum(jnp.square(queries), axis=-1), jnp.sum(jnp.square(key_cols), axis=-1)), "seq"
    )
    full_width = local_width * lax.axis_size("seq")
    qk_gains = qk_gain[0]
    query_scale = lax.rsqrt(square_sums[0] / full_width + epsilon)[:, None]
    key_scale = lax.rsqrt(square_sums[1] / full_width + epsilon)[:, None]
    query_normed = (queries * query_scale * qk_gains[0]).astype(jnp.bfloat16)
    key_normed = (key_cols * key_scale * qk_gains[1]).astype(jnp.bfloat16)
    value_normed = value_cols.astype(jnp.bfloat16)
    section_index = lax.axis_index("pipe")
    patch_slot = jnp.mod(patch_index[0] - section_index, NPATCH)
    first_row = patch_slot * patch_tokens
    key_set = lax.dynamic_update_slice(stale_kv[0, 0, 0], key_normed, (first_row, jnp.int32(0)))
    value_set = lax.dynamic_update_slice(stale_kv[0, 0, 1], value_normed, (first_row, jnp.int32(0)))
    seq_rows = key_set.shape[0]
    heads_here = local_width // HEAD
    key_heads = key_set.reshape(seq_rows, heads_here, HEAD)
    value_heads = value_set.reshape(seq_rows, heads_here, HEAD)
    block_rows = math.gcd(patch_tokens, 512)
    block_count = patch_tokens // block_rows

    def attend(query_block):
        scores = jnp.einsum(
            "qhc,khc->hqk", query_block, key_heads, preferred_element_type=jnp.float32
        ) * HEAD ** (-0.5)
        top = jnp.max(scores, axis=-1, keepdims=True)
        expo = jnp.exp(scores - top)
        weights = (expo / jnp.sum(expo, axis=-1, keepdims=True)).astype(jnp.bfloat16)
        mixed = jnp.einsum("hqk,khc->qhc", weights, value_heads, preferred_element_type=jnp.float32)
        return mixed.astype(jnp.bfloat16).reshape(block_rows, local_width)

    attended = lax.map(attend, query_normed.reshape(block_count, block_rows, heads_here, HEAD))
    attended = attended.reshape(patch_tokens, local_width)
    out_rows = out_weight[0]
    projected = lax.psum_scatter(
        jnp.dot(attended, out_rows, preferred_element_type=jnp.float32).astype(jnp.bfloat16),
        "seq",
        scatter_dimension=0,
        tiled=True,
    ).astype(jnp.float32)
    block_out = (tokens_in.astype(jnp.float32) + mod_rows[2] * projected).astype(jnp.bfloat16)
    forwarded = passed_along(block_out, "pipe", 1)
    normed_out = modulate(block_out, head_rows[0], head_rows[1]).astype(jnp.bfloat16)
    readout = jnp.dot(normed_out, head_weight, preferred_element_type=jnp.float32)
    branch_index = lax.axis_index("cfg")
    half_width = readout.shape[1] // 2
    partner = partner_2(readout.astype(jnp.bfloat16), "cfg", 0).astype(readout.dtype)
    conditional = jnp.where(branch_index == 0, readout, partner)
    unconditional = jnp.where(branch_index == 0, partner, readout)
    combined = unconditional + guidance * (conditional - unconditional)
    guided = lax.dynamic_slice_in_dim(combined, branch_index * half_width, half_width, 1)
    fresh_pair = jnp.stack([key_normed, value_normed])
    return (forwarded[None, None], fresh_pair[None, None], guided[None])


def solution(mesh):
    return jax.shard_map(
        per_device,
        mesh=mesh,
        in_specs=(
            P("cfg", "pipe", "seq", None),
            P("pipe", None, None, "seq"),
            P("pipe", "seq", None),
            P("pipe", None, "seq"),
            P("cfg", "pipe", None, None, "seq"),
            P("pipe", None, None, None),
            P(),
            P(),
            P(),
            P(),
        ),
        out_specs=(
            P("cfg", "pipe", "seq", None),
            P("cfg", "pipe", None, None, "seq"),
            P("pipe", "seq", "cfg"),
        ),
        check_vma=False,
    )
```

profile of v0, /device:TPU:0, one launch (start us, length us, event | category | flops | bytes accessed | tf_op | source)
XLA Modules:
  0.0 539.0 jit_solution(13400286598347990033)
XLA Ops:
  12.8 2.9 fusion.38
  16.5 10.7 %copy.18 = bf16[1,5120,3,256]{1,3,2,0:T(8,128)(2,1)} copy(bf16[1,5120,3,256]{3,1,2,0:T(8,128)(2,1)} %param.13) | data formatting | bytes 15728640 | tf_op args[1]
  27.3 5.1 slice_bitcast_fusion
  32.4 4.1 copy.28
  36.5 114.6 %all-gather.2.cloned.1.call-done = bf16[2048,5120]{1,0:T(8,128)(2,1)} async-done(((bf16[128,5120]{1,0:T(8,128)(2,1)}), bf16[2048,5120]{1,0:T(8,128)(2,1)}) %all-gather.2.cloned.1.call-update) | async-done | bytes 20971536 | tf_op jit(solution)/shard_map/all_gather | solution.py:52
  151.0 20.4 %fusion.57 = f32[2048,768]{0,1:T(8,128)S(1)} fusion(bf16[2048,5120]{1,0:T(8,128)(2,1)} %all-gather.2.cloned.1.call-done, bf16[5120,768]{0,1:T(8,128)(2,1)} %bitcast.88), kind=kOutput, calls=%fused_computation.71 | convolution fusion | flops 16106127360 | bytes 35127296 | tf_op jit(solution)/shard_map/dot_general | solution.py:51
  171.4 2.7 copy-done.1
  174.5 72.4 %all-reduce = (f32[2048]{0:T(1024)S(1)}, f32[2048]{0:T(1024)S(1)}) all-reduce(f32[2048]{0:T(1024)S(1)} %get-tuple-element.48, f32[2048]{0:T(1024)S(1)} %get-tuple-element.47), channel_id=1, replica_groups=mesh['pipe'=4,'seq'=16,'cfg'=2] {'seq'}, use_global_device_ids=true, to_apply=%region_3.4 | all-reduce | flops 4096 | bytes 32768 | tf_op jit(solution)/shard_map/psum | solution.py:60
  246.9 3.8 fusion.54
  250.7 2.3 copy.20
  253.0 2.3 constant_dynamic-update-slice_fusion.1
  255.2 4.1 copy.21
  259.3 4.1 copy.23
  263.4 4.0 fusion.47
  267.4 2.6 reshape.79
  270.0 2.6 copy.22
  272.7 82.0 %while.10 = (s32[]{:T(128)}, bf16[4,512,256]{2,1,0:T(8,128)(2,1)}, bf16[4,512,2,128]{3,1,2,0:T(8,128)(2,1)}, bf16[4096,2,128]{2,0,1:T(8,128)(2,1)}, bf16[4096,2,128]{0,2,1:T(8,128)(2,1)}, /*index=5*/s32[]{:T(128)}) while((s32[]{:T(128)}, bf16[4,512,256]{2,1,0:T(8,128)(2,1)}, bf16[4,512,2,128]{3,1,2,0:T(8,128)(2,1)}, ...), condition=%wide.region_9.10_spmd, body=%wide.region_6.9_spmd.sunk | while | flops 2168590336 | bytes 39330884 | solution.py:92
  272.7 10.3 %fusion.73 = (f32[2,512]{1,0:T(2,128)S(1)}, f32[2,512,4096]{2,1,0:T(8,128)}) fusion(bf16[4096,2,128]{2,0,1:T(8,128)(2,1)} %get-tuple-element.132, bf16[4,512,2,128]{3,1,2,0:T(8,128)(2,1)} %get-tuple-element.131, s32[]{:T(128)} %get-tuple-element.123), kind=kOutput, calls=%fused_computation.67.clone.1 | convolution fusion | flops 1086328832 | bytes 19141120 | tf_op jit(solution)/shard_map/while/body/eval_jaxpr/sub | solution.py:87
  282.9 9.3 %fusion.74 = bf16[2,512,128]{1,2,0:T(8,128)(2,1)S(1)} fusion(bf16[4096,2,128]{0,2,1:T(8,128)(2,1)} %get-tuple-element.133, f32[2,512,4096]{2,1,0:T(8,128)} %get-tuple-element.115, f32[2,512]{1,0:T(2,128)S(1)} %get-tuple-element.116), kind=kOutput, calls=%fused_computation.8.clone.1 | convolution fusion | flops 1082261504 | bytes 19140608 | tf_op jit(solution)/shard_map/while/body/eval_jaxpr/hqk,khc->qhc/dot_general | solution.py:89
  293.2 10.3 %fusion.73 = (f32[2,512]{1,0:T(2,128)S(1)}, f32[2,512,4096]{2,1,0:T(8,128)}) fusion(bf16[4096,2,128]{2,0,1:T(8,128)(2,1)} %get-tuple-element.132, bf16[4,512,2,128]{3,1,2,0:T(8,128)(2,1)} %get-tuple-element.131, s32[]{:T(128)} %get-tuple-element.123), kind=kOutput, calls=%fused_computation.67.clone.1 | convolution fusion | flops 1086328832 | bytes 19141120 | tf_op jit(solution)/shard_map/while/body/eval_jaxpr/sub | solution.py:87
  303.4 9.3 %fusion.74 = bf16[2,512,128]{1,2,0:T(8,128)(2,1)S(1)} fusion(bf16[4096,2,128]{0,2,1:T(8,128)(2,1)} %get-tuple-element.133, f32[2,512,4096]{2,1,0:T(8,128)} %get-tuple-element.115, f32[2,512]{1,0:T(2,128)S(1)} %get-tuple-element.116), kind=kOutput, calls=%fused_computation.8.clone.1 | convolution fusion | flops 1082261504 | bytes 19140608 | tf_op jit(solution)/shard_map/while/body/eval_jaxpr/hqk,khc->qhc/dot_general | solution.py:89
  313.7 10.3 %fusion.73 = (f32[2,512]{1,0:T(2,128)S(1)}, f32[2,512,4096]{2,1,0:T(8,128)}) fusion(bf16[4096,2,128]{2,0,1:T(8,128)(2,1)} %get-tuple-element.132, bf16[4,512,2,128]{3,1,2,0:T(8,128)(2,1)} %get-tuple-element.131, s32[]{:T(128)} %get-tuple-element.123), kind=kOutput, calls=%fused_computation.67.clone.1 | convolution fusion | flops 1086328832 | bytes 19141120 | tf_op jit(solution)/shard_map/while/body/eval_jaxpr/sub | solution.py:87
  323.9 9.3 %fusion.74 = bf16[2,512,128]{1,2,0:T(8,128)(2,1)S(1)} fusion(bf16[4096,2,128]{0,2,1:T(8,128)(2,1)} %get-tuple-element.133, f32[2,512,4096]{2,1,0:T(8,128)} %get-tuple-element.115, f32[2,512]{1,0:T(2,128)S(1)} %get-tuple-element.116), kind=kOutput, calls=%fused_computation.8.clone.1 | convolution fusion | flops 1082261504 | bytes 19140608 | tf_op jit(solution)/shard_map/while/body/eval_jaxpr/hqk,khc->qhc/dot_general | solution.py:89
  334.1 10.3 %fusion.73 = (f32[2,512]{1,0:T(2,128)S(1)}, f32[2,512,4096]{2,1,0:T(8,128)}) fusion(bf16[4096,2,128]{2,0,1:T(8,128)(2,1)} %get-tuple-element.132, bf16[4,512,2,128]{3,1,2,0:T(8,128)(2,1)} %get-tuple-element.131, s32[]{:T(128)} %get-tuple-element.123), kind=kOutput, calls=%fused_computation.67.clone.1 | convolution fusion | flops 1086328832 | bytes 19141120 | tf_op jit(solution)/shard_map/while/body/eval_jaxpr/sub | solution.py:87
  344.4 9.4 %fusion.74 = bf16[2,512,128]{1,2,0:T(8,128)(2,1)S(1)} fusion(bf16[4096,2,128]{0,2,1:T(8,128)(2,1)} %get-tuple-element.133, f32[2,512,4096]{2,1,0:T(8,128)} %get-tuple-element.115, f32[2,512]{1,0:T(2,128)S(1)} %get-tuple-element.116), kind=kOutput, calls=%fused_computation.8.clone.1 | convolution fusion | flops 1082261504 | bytes 19140608 | tf_op jit(solution)/shard_map/while/body/eval_jaxpr/hqk,khc->qhc/dot_general | solution.py:89
  354.6 11.2 %convolution_convert_fusion = bf16[2048,5120]{1,0:T(8,128)(2,1)} fusion(bf16[2048,256]{1,0:T(8,128)(2,1)} %bitcast.91, bf16[1,256,5120]{2,1,0:T(8,128)(2,1)S(1)} %copy-done), kind=kOutput, calls=%fused_computation.18 | convolution fusion | flops 5379194880 | bytes 24641536 | tf_op jit(solution)/shard_map/dot_general | solution.py:96
  366.8 127.4 %reduce-scatter.2.cloned.1.call-done = bf16[128,5120]{1,0:T(8,128)(2,1)} async-done(((bf16[2048,5120]{1,0:T(8,128)(2,1)}), bf16[128,5120]{1,0:T(8,128)(2,1)}) %reduce-scatter.2.cloned.1.call-update) | async-done | bytes 1310736 | tf_op jit(solution)/shard_map/reduce_scatter | solution.py:95
  494.2 3.3 convert_reduce_fusion
  501.1 2.1 fusion.56
  504.8 3.9 copy.25
  509.4 20.3 %collective-permute-done = bf16[128,5120]{1,0:T(8,128)(2,1)} collective-permute-done((bf16[128,5120]{1,0:T(8,128)(2,1)}, bf16[128,5120]{1,0:T(8,128)(2,1)}, u32[]{:S(2)}, u32[]{:S(2)}) %collective-permute-start) | collective-permute-done | bytes 1310752 | tf_op jit(solution)/shard_map/ppermute | solution.py:16
  529.7 2.5 copy.43
  (43 shorter events, 15.5 us)
Async XLA Ops:
  7.2 347.5 %copy-start = (bf16[1,256,5120]{2,1,0:T(8,128)(2,1)S(1)}, bf16[1,256,5120]{2,1,0:T(8,128)(2,1)}, u32[]{:S(2)}) copy-start(bf16[1,256,5120]{2,1,0:T(8,128)(2,1)} %param.14) | copy-start | bytes 7864324
  7.2 143.8 %all-gather.2.cloned.1.call-start = ((), (), s32[]{:S(2)}) async-start(), calls=%async_computation.1 | async-start | bytes 22282240 | tf_op jit(solution)/shard_map/all_gather | solution.py:52
  15.8 478.4 %reduce-scatter.2.cloned.1.call-start = ((), (), s32[]{:S(2)}) async-start(), calls=%async_computation.2 | async-start | bytes 22282240 | tf_op jit(solution)/shard_map/reduce_scatter | solution.py:95
  32.4 4.1 copy-start.5
  171.4 2.7 copy-start.1
  365.9 128.4 %copy-start.4 = (f32[1,1,1,5120]{3,0,2,1:T(1,128)S(1)}, f32[1,1,1,5120]{3,0,2,1:T(1,128)}, u32[]{:S(2)}) copy-start(f32[1,1,1,5120]{3,0,2,1:T(1,128)} %get-tuple-element.71) | copy-start | bytes 61444
  494.2 6.8 %copy-start.6 = (bf16[5120,64]{0,1:T(8,128)(2,1)S(1)}, bf16[5120,64]{0,1:T(8,128)(2,1)}, u32[]{:S(2)}) copy-start(bf16[5120,64]{0,1:T(8,128)(2,1)} %param.19) | copy-start | bytes 1966084
  497.5 32.1 %collective-permute-start = (bf16[128,5120]{1,0:T(8,128)(2,1)}, bf16[128,5120]{1,0:T(8,128)(2,1)}, u32[]{:S(2)}, u32[]{:S(2)}) collective-permute-start(bf16[128,5120]{1,0:T(8,128)(2,1)} %get-tuple-element.62), channel_id=1, source_target_pairs={{96,0},{0,32},{32,64},{64,96},{97,1},{1,33},{33,65},{65,97},{98,2}... | collective-permute-start | bytes 3932168 | tf_op jit(solution)/shard_map/ppermute | solution.py:16
  499.1 4.2 copy-start.2
  499.1 4.2 copy-start.3
  503.2 5.6 %collective-permute-start.1 = (bf16[128,64]{0,1:T(8,128)(2,1)S(1)}, bf16[128,64]{0,1:T(8,128)(2,1)S(1)}, u32[]{:S(2)}, u32[]{:S(2)}) collective-permute-start(bf16[128,64]{0,1:T(8,128)(2,1)S(1)} %get-tuple-element.78), channel_id=1, source_target_pairs={{0,1},{1,0},{2,3},{3,2},{4,5},{5,4},{6,7},{7,6},{8,9},{9,8},{10,11... | collective-permute-start | bytes 49160 | tf_op jit(solution)/shard_map/ppermute | solution.py:20
Sparse Core Ops, SparseCore 0:
  15.9 135.0 all-gather.1
  366.0 128.1 reduce-scatter.1
where the time goes:
time: 540 us; the launch traced here: 539 us
  waiting for transfers between devices  262 us (49%)
  matrix products  112 us (21%)
  blocking collectives  72.4 us (13%)
  local copies, waits for them, and re-layouts  50.4 us (9%)
  other arithmetic  24.3 us (4%)
  between operations  15.6 us (3%)
    reduce_scatter x1, waiting for transfers between devices, per_device(): lax.psum_scatter(jnp.dot(attended, out_rows, preferred_element_type=jnp.f...  127 us
    all_gather x1, waiting for transfers between devices, per_device(): lax.all_gather(normed, 'seq', axis=0, tiled=True)  115 us
    psum x1, blocking collectives, per_device(): lax.psum((jnp.sum(jnp.square(queries), axis=-1), jnp.sum(jnp.square(key_c...  72.4 us
    sub x4, matrix products, attend(): expo = jnp.exp(scores - top)  41.1 us
    dot_general x4, matrix products, attend(): jnp.einsum('hqk,khc->qhc', weights, value_heads, preferred_element_type=j...  37.4 us
    unnamed x18, local copies, waits for them, and re-layouts  23.9 us
    dot_general x1, matrix products, per_device(): jnp.dot(lax.all_gather(normed, 'seq', axis=0, tiled=True), in_weight, pre...  20.4 us
    ppermute x1, waiting for transfers between devices, passed_along(): return lax.ppermute(block, axis, route)  20.3 us
  transfers between devices with their start and end apart: 4, of which 3 were waited for; matrix products, arithmetic and copies ran while one was open for 6% of the time, Pallas kernels for 0%

commit v1 on v0

--- a/solution.py
+++ b/solution.py
@@ -49,7 +49,9 @@
     in_weight = in_weight.reshape(model_width, 3 * local_width)
     normed = modulate(tokens_in, mod_rows[0], mod_rows[1]).astype(jnp.bfloat16)
     projections = jnp.dot(
-        lax.all_gather(normed, "seq", axis=0, tiled=True),
+        jnp.concatenate(
+            lax.all_to_all(jnp.stack([normed] * lax.axis_size("seq")), "seq", 0, 0), axis=0
+        ),
         in_weight,
         preferred_element_type=jnp.float32,
     )

time: 540 us -> 730 us (1.35)
  waiting for transfers between devices: 262 us -> 441 us
    all_to_all x0 -> x1, waiting for transfers between devices: none -> 293 us  [per_device(): lax.all_to_all(jnp.stack([normed] * lax.axis_size('seq')), 'seq', 0, 0)]
    all_gather x1 -> x0, waiting for transfers between devices: 115 us -> none  [per_device(): lax.all_gather(normed, 'seq', axis=0, tiled=True)]
    another operation x0 -> x1, local copies, waits for them, and re-layouts: none -> 7.41 us  [per_device(): jnp.stack([normed] * lax.axis_size('seq'))]
  transfers between devices with their start and end apart: 4 -> 4, of which waited for: 3 -> 3; matrix products, arithmetic and copies ran while one was open for 6% -> 4% of each run, Pallas kernels for 0% -> 0%
where the time goes in v1:
time: 730 us; the launch traced here: 728 us
  waiting for transfers between devices  441 us (60%)
  matrix products  112 us (15%)
  blocking collectives  70.1 us (10%)
  local copies, waits for them, and re-layouts  57.2 us (8%)
  other arithmetic  23.2 us (3%)
  between operations  15.6 us (2%)
  starting transfers between devices  8.86 us (1%)
    all_to_all x1, waiting for transfers between devices, per_device(): lax.all_to_all(jnp.stack([normed] * lax.axis_size('seq')), 'seq', 0, 0)  293 us
    reduce_scatter x1, waiting for transfers between devices, per_device(): lax.psum_scatter(jnp.dot(attended, out_rows, preferred_element_type=jnp.f...  128 us
    psum x1, blocking collectives, per_device(): lax.psum((jnp.sum(jnp.square(queries), axis=-1), jnp.sum(jnp.square(key_c...  70.1 us
    sub x4, matrix products, attend(): expo = jnp.exp(scores - top)  41.1 us
    dot_general x4, matrix products, attend(): jnp.einsum('hqk,khc->qhc', weights, value_heads, preferred_element_type=j...  37.4 us
    unnamed x18, local copies, waits for them, and re-layouts  23.9 us
    dot_general x1, matrix products, per_device(): jnp.dot(jnp.concatenate(lax.all_to_all(jnp.stack([normed] * lax.axis_size...  20.4 us
    ppermute x1, waiting for transfers between devices, passed_along(): return lax.ppermute(block, axis, route)  20.3 us
  transfers between devices with their start and end apart: 4, of which 3 were waited for; matrix products, arithmetic and copies ran while one was open for 4% of the time, Pallas kernels for 0%

profile of v1, /device:TPU:0, one launch (start us, length us, event | category | flops | bytes accessed | tf_op | source)
XLA Modules:
  0.0 728.5 jit_solution(8972580006647074403)
XLA Ops:
  14.7 7.4 %stack.8 = bf16[16,128,5120]{2,1,0:T(8,128)(2,1)} broadcast(bf16[128,5120]{1,0:T(8,128)(2,1)S(1)} %fusion.38), dimensions={1,2} | broadcast | bytes 22282240 | tf_op jit(solution)/shard_map/stack | solution.py:53
  22.1 7.2 all-to-all-start
  30.0 10.7 %copy.18 = bf16[1,5120,3,256]{1,3,2,0:T(8,128)(2,1)} copy(bf16[1,5120,3,256]{3,1,2,0:T(8,128)(2,1)} %param.13) | data formatting | bytes 15728640 | tf_op args[1]
  40.7 4.5 slice_bitcast_fusion
  45.2 4.1 copy.28
  49.3 292.7 %all-to-all-done = bf16[16,128,5120]{2,1,0:T(8,128)(2,1)} async-done(((bf16[16,128,5120]{2,1,0:T(8,128)(2,1)}), bf16[16,128,5120]{2,1,0:T(8,128)(2,1)}, u32[]{:S(2)}, u32[]{:S(2)}) %all-to-all-start) | async-done | bytes 20971552 | tf_op jit(solution)/shard_map/all_to_all | solution.py:53
  342.0 20.4 %fusion.57 = f32[2048,768]{0,1:T(8,128)S(1)} fusion(bf16[2048,5120]{1,0:T(8,128)(2,1)} %bitcast.8, bf16[5120,768]{0,1:T(8,128)(2,1)} %bitcast.89), kind=kOutput, calls=%fused_computation.71 | convolution fusion | flops 16106127360 | bytes 35127296 | tf_op jit(solution)/shard_map/dot_general | solution.py:51
  362.4 2.7 copy-done.1
  365.4 70.1 %all-reduce = (f32[2048]{0:T(1024)S(1)}, f32[2048]{0:T(1024)S(1)}) all-reduce(f32[2048]{0:T(1024)S(1)} %get-tuple-element.48, f32[2048]{0:T(1024)S(1)} %get-tuple-element.47), channel_id=1, replica_groups=mesh['pipe'=4,'seq'=16,'cfg'=2] {'seq'}, use_global_device_ids=true, to_apply=%region_3.4 | all-reduce | flops 4096 | bytes 32768 | tf_op jit(solution)/shard_map/psum | solution.py:62
  435.5 3.8 fusion.54
  439.3 2.3 copy.20
  441.6 2.3 constant_dynamic-update-slice_fusion.1
  443.9 4.1 copy.21
  448.0 4.1 copy.23
  452.0 4.0 fusion.47
  456.0 2.6 reshape.119
  458.6 2.6 copy.22
  461.3 82.0 %while.10 = (s32[]{:T(128)}, bf16[4,512,256]{2,1,0:T(8,128)(2,1)}, bf16[4,512,2,128]{3,1,2,0:T(8,128)(2,1)}, bf16[4096,2,128]{2,0,1:T(8,128)(2,1)}, bf16[4096,2,128]{0,2,1:T(8,128)(2,1)}, /*index=5*/s32[]{:T(128)}) while((s32[]{:T(128)}, bf16[4,512,256]{2,1,0:T(8,128)(2,1)}, bf16[4,512,2,128]{3,1,2,0:T(8,128)(2,1)}, ...), condition=%wide.region_9.10_spmd, body=%wide.region_6.9_spmd.sunk | while | flops 2168590336 | bytes 39330884 | solution.py:94
  461.3 10.3 %fusion.73 = (f32[2,512]{1,0:T(2,128)S(1)}, f32[2,512,4096]{2,1,0:T(8,128)}) fusion(bf16[4096,2,128]{2,0,1:T(8,128)(2,1)} %get-tuple-element.132, bf16[4,512,2,128]{3,1,2,0:T(8,128)(2,1)} %get-tuple-element.131, s32[]{:T(128)} %get-tuple-element.123), kind=kOutput, calls=%fused_computation.67.clone.1 | convolution fusion | flops 1086328832 | bytes 19141120 | tf_op jit(solution)/shard_map/while/body/eval_jaxpr/sub | solution.py:89
  471.6 9.3 %fusion.74 = bf16[2,512,128]{1,2,0:T(8,128)(2,1)S(1)} fusion(bf16[4096,2,128]{0,2,1:T(8,128)(2,1)} %get-tuple-element.133, f32[2,512,4096]{2,1,0:T(8,128)} %get-tuple-element.115, f32[2,512]{1,0:T(2,128)S(1)} %get-tuple-element.116), kind=kOutput, calls=%fused_computation.8.clone.1 | convolution fusion | flops 1082261504 | bytes 19140608 | tf_op jit(solution)/shard_map/while/body/eval_jaxpr/hqk,khc->qhc/dot_general | solution.py:91
  481.8 10.3 %fusion.73 = (f32[2,512]{1,0:T(2,128)S(1)}, f32[2,512,4096]{2,1,0:T(8,128)}) fusion(bf16[4096,2,128]{2,0,1:T(8,128)(2,1)} %get-tuple-element.132, bf16[4,512,2,128]{3,1,2,0:T(8,128)(2,1)} %get-tuple-element.131, s32[]{:T(128)} %get-tuple-element.123), kind=kOutput, calls=%fused_computation.67.clone.1 | convolution fusion | flops 1086328832 | bytes 19141120 | tf_op jit(solution)/shard_map/while/body/eval_jaxpr/sub | solution.py:89
  492.0 9.4 %fusion.74 = bf16[2,512,128]{1,2,0:T(8,128)(2,1)S(1)} fusion(bf16[4096,2,128]{0,2,1:T(8,128)(2,1)} %get-tuple-element.133, f32[2,512,4096]{2,1,0:T(8,128)} %get-tuple-element.115, f32[2,512]{1,0:T(2,128)S(1)} %get-tuple-element.116), kind=kOutput, calls=%fused_computation.8.clone.1 | convolution fusion | flops 1082261504 | bytes 19140608 | tf_op jit(solution)/shard_map/while/body/eval_jaxpr/hqk,khc->qhc/dot_general | solution.py:91
  502.3 10.3 %fusion.73 = (f32[2,512]{1,0:T(2,128)S(1)}, f32[2,512,4096]{2,1,0:T(8,128)}) fusion(bf16[4096,2,128]{2,0,1:T(8,128)(2,1)} %get-tuple-element.132, bf16[4,512,2,128]{3,1,2,0:T(8,128)(2,1)} %get-tuple-element.131, s32[]{:T(128)} %get-tuple-element.123), kind=kOutput, calls=%fused_computation.67.clone.1 | convolution fusion | flops 1086328832 | bytes 19141120 | tf_op jit(solution)/shard_map/while/body/eval_jaxpr/sub | solution.py:89
  512.5 9.3 %fusion.74 = bf16[2,512,128]{1,2,0:T(8,128)(2,1)S(1)} fusion(bf16[4096,2,128]{0,2,1:T(8,128)(2,1)} %get-tuple-element.133, f32[2,512,4096]{2,1,0:T(8,128)} %get-tuple-element.115, f32[2,512]{1,0:T(2,128)S(1)} %get-tuple-element.116), kind=kOutput, calls=%fused_computation.8.clone.1 | convolution fusion | flops 1082261504 | bytes 19140608 | tf_op jit(solution)/shard_map/while/body/eval_jaxpr/hqk,khc->qhc/dot_general | solution.py:91
  522.8 10.3 %fusion.73 = (f32[2,512]{1,0:T(2,128)S(1)}, f32[2,512,4096]{2,1,0:T(8,128)}) fusion(bf16[4096,2,128]{2,0,1:T(8,128)(2,1)} %get-tuple-element.132, bf16[4,512,2,128]{3,1,2,0:T(8,128)(2,1)} %get-tuple-element.131, s32[]{:T(128)} %get-tuple-element.123), kind=kOutput, calls=%fused_computation.67.clone.1 | convolution fusion | flops 1086328832 | bytes 19141120 | tf_op jit(solution)/shard_map/while/body/eval_jaxpr/sub | solution.py:89
  533.0 9.4 %fusion.74 = bf16[2,512,128]{1,2,0:T(8,128)(2,1)S(1)} fusion(bf16[4096,2,128]{0,2,1:T(8,128)(2,1)} %get-tuple-element.133, f32[2,512,4096]{2,1,0:T(8,128)} %get-tuple-element.115, f32[2,512]{1,0:T(2,128)S(1)} %get-tuple-element.116), kind=kOutput, calls=%fused_computation.8.clone.1 | convolution fusion | flops 1082261504 | bytes 19140608 | tf_op jit(solution)/shard_map/while/body/eval_jaxpr/hqk,khc->qhc/dot_general | solution.py:91
  543.3 11.2 %convolution_convert_fusion = bf16[2048,5120]{1,0:T(8,128)(2,1)} fusion(bf16[2048,256]{1,0:T(8,128)(2,1)} %bitcast.92, bf16[1,256,5120]{2,1,0:T(8,128)(2,1)S(1)} %copy-done), kind=kOutput, calls=%fused_computation.18 | convolution fusion | flops 5379194880 | bytes 24641536 | tf_op jit(solution)/shard_map/dot_general | solution.py:98
  555.4 128.3 %reduce-scatter.2.cloned.1.call-done = bf16[128,5120]{1,0:T(8,128)(2,1)} async-done(((bf16[2048,5120]{1,0:T(8,128)(2,1)}), bf16[128,5120]{1,0:T(8,128)(2,1)}) %reduce-scatter.2.cloned.1.call-update) | async-done | bytes 1310736 | tf_op jit(solution)/shard_map/reduce_scatter | solution.py:97
  683.8 3.3 convert_reduce_fusion
  694.4 3.9 copy.25
  698.9 20.3 %collective-permute-done = bf16[128,5120]{1,0:T(8,128)(2,1)} collective-permute-done((bf16[128,5120]{1,0:T(8,128)(2,1)}, bf16[128,5120]{1,0:T(8,128)(2,1)}, u32[]{:S(2)}, u32[]{:S(2)}) %collective-permute-start) | collective-permute-done | bytes 1310752 | tf_op jit(solution)/shard_map/ppermute | solution.py:16
  719.2 2.5 copy.43
  (43 shorter events, 19.4 us)
Async XLA Ops:
  7.2 536.1 %copy-start = (bf16[1,256,5120]{2,1,0:T(8,128)(2,1)S(1)}, bf16[1,256,5120]{2,1,0:T(8,128)(2,1)}, u32[]{:S(2)}) copy-start(bf16[1,256,5120]{2,1,0:T(8,128)(2,1)} %param.14) | copy-start | bytes 7864324
  22.1 319.9 %all-to-all-start = ((bf16[16,128,5120]{2,1,0:T(8,128)(2,1)}), bf16[16,128,5120]{2,1,0:T(8,128)(2,1)}, u32[]{:S(2)}, u32[]{:S(2)}) async-start(bf16[16,128,5120]{2,1,0:T(8,128)(2,1)} %stack.8), calls=%async_computation | async-start | bytes 41943040 | tf_op jit(solution)/shard_map/all_to_all | solution.py:53
  29.3 654.5 %reduce-scatter.2.cloned.1.call-start = ((), (), s32[]{:S(2)}) async-start(), calls=%async_computation.2 | async-start | bytes 22282240 | tf_op jit(solution)/shard_map/reduce_scatter | solution.py:97
  45.2 4.1 copy-start.5
  362.4 2.7 copy-start.1
  554.5 129.2 %copy-start.4 = (f32[1,1,1,5120]{3,0,2,1:T(1,128)S(1)}, f32[1,1,1,5120]{3,0,2,1:T(1,128)}, u32[]{:S(2)}) copy-start(f32[1,1,1,5120]{3,0,2,1:T(1,128)} %get-tuple-element.71) | copy-start | bytes 61444
  683.8 6.9 copy-start.6
  687.1 32.1 %collective-permute-start = (bf16[128,5120]{1,0:T(8,128)(2,1)}, bf16[128,5120]{1,0:T(8,128)(2,1)}, u32[]{:S(2)}, u32[]{:S(2)}) collective-permute-start(bf16[128,5120]{1,0:T(8,128)(2,1)} %get-tuple-element.62), channel_id=1, source_target_pairs={{96,0},{0,32},{32,64},{64,96},{97,1},{1,33},{33,65},{65,97},{98,2}... | collective-permute-start | bytes 3932168 | tf_op jit(solution)/shard_map/ppermute | solution.py:16
  688.6 4.2 copy-start.2
  688.6 4.2 copy-start.3
  692.7 5.6 collective-permute-start.1
Sparse Core Ops, SparseCore 0:
  554.7 129.0 reduce-scatter.1
